TPU v7x, 32 devices: a whole 2x2x4 slice. The times are simulated.
32 devices in a mesh: section: 4 (over x, core), seq: 8 (over z, y).
Axes of the slice: x: 2, y: 2, z: 4, core: 2. Of those that a mesh axis runs over, the one named last changes fastest.
Arguments:
- hidden: bfloat16 [2, 1024, 2688], P(None, 'seq'), may hold values from -6 to 6
- lengths: int32 [2], replicated, may hold values from 512 to 1024, as said below
- reward_pos: int32 [2], replicated, may hold values from 384 to 1023, as said below
- in_gain: bfloat16 [2688], P('seq'), may hold values from 0.099609375 to 1.8984375
- w_query: bfloat16 [2688, 2048], P('seq', 'section'), may hold values from -0.077151675 to 0.077151675
- w_key: bfloat16 [2688, 1024], P('seq', 'section'), may hold values from -0.077151675 to 0.077151675
- w_value: bfloat16 [2688, 1024], P('seq', 'section'), may hold values from -0.125 to 0.125
- query_gain: float32 [128], replicated, may hold values from 0.6 to 7
- key_gain: float32 [128], replicated, may hold values from 0.6 to 7
- w_out: bfloat16 [2048, 2688], P('section', 'seq'), may hold values from -0.125 to 0.125
- post_gain: bfloat16 [2688], P('seq'), may hold values from 0.099609375 to 1.8984375
- final_gain: bfloat16 [2688], P('seq'), may hold values from 0.099609375 to 1.8984375
- value_head: bfloat16 [2688], P('seq'), may hold values from -0.125 to 0.125
Outputs:
- token_values: float32 [2, 1024], P(None, 'seq')
- reward: float32 [2], replicated
Inputs may be any that keep to these rules, and one draw needn't show every extreme that they name: `lengths`: in every draw at least one micro-batch has all 1024 tokens valid. reward_pos[m] lies among the last 128 valid tokens of micro-batch m.
All inputs are finite; a program needn't handle non-finite values.
Results may differ from a plain program's by a relative error of at most 0.01.
Values may be sent and summed in bfloat16 or wider, within the bound.
A program may use at most 64 MiB of HBM per device.

v0:
```python
import jax
import jax.numpy as jnp
from jax import lax
from jax.sharding import PartitionSpec as P

HD = 128
GROUP = 2
WINDOW = 1024


norm_eps = 1e-06
query_scale = 168.0 ** (-0.5)
rope_base = 10000.0


def passed_along(array, axis, by):
    devices = lax.axis_size(axis)
    pairs = [(i, i + by) for i in range(devices) if 0 <= i + by < devices]
    return lax.ppermute(array, axis, pairs)


def rms_scale(values, gain_vec):
    return (
        values * lax.rsqrt(jnp.mean(values * values, axis=-1, keepdims=True) + norm_eps) * gain_vec
    )


def rotate_pairs(head_rows, positions):
    half_width = head_rows.shape[-1] // 2
    frequency = rope_base ** (
        -jnp.arange(half_width, dtype=jnp.float32) * 2.0 / head_rows.shape[-1]
    )
    angles = positions.astype(jnp.float32)[:, None] * frequency[None, :]
    target = (angles.shape[0],) + (1,) * (head_rows.ndim - 2) + (half_width,)
    cosine = jnp.cos(angles).reshape(target)
    sine_part = jnp.sin(angles).reshape(target)
    front_half = head_rows[..., :half_width]
    back_half = head_rows[..., half_width:]
    return jnp.concatenate(
        [front_half * cosine - back_half * sine_part, back_half * cosine + front_half * sine_part],
        axis=-1,
    )


def window_blocks(packed, tok_dev):
    block_count = WINDOW // tok_dev + 1
    blocks_held = [packed]
    for offset in range(1, block_count):
        blocks_held.append(passed_along(packed, "seq", offset))
    return jnp.concatenate(blocks_held[::-1], axis=1)


def window_attention(queries, keys_all, values_all, query_pos, key_pos):
    scores = jnp.einsum("qhgd,khd->hgqk", queries, keys_all, preferred_element_type=jnp.float32)
    allowed = (
        (key_pos[None, :] <= query_pos[:, None])
        & (key_pos[None, :] > query_pos[:, None] - WINDOW)
        & (key_pos[None, :] >= 0)
    )
    scores = jnp.where(allowed[None, None], scores, -1e30)
    row_top = jnp.max(scores, axis=-1, keepdims=True)
    exponent = jnp.exp(scores - row_top)
    attn_weights = (exponent / jnp.sum(exponent, axis=-1, keepdims=True)).astype(jnp.bfloat16)
    mixed_heads = jnp.einsum(
        "hgqk,khd->qhgd", attn_weights, values_all, preferred_element_type=jnp.float32
    )
    return mixed_heads.astype(jnp.bfloat16)


def local(
    hidden,
    lengths,
    reward_pos,
    in_gain,
    w_query,
    w_key,
    w_value,
    query_gain,
    key_gain,
    w_out,
    post_gain,
    final_gain,
    value_head,
):
    micro_count, tok_dev, width = hidden.shape
    row_count = micro_count * tok_dev
    qwidth = w_query.shape[1]
    kwidth = w_key.shape[1]
    heads_here = kwidth // HD
    widened = hidden.reshape(row_count, width).astype(jnp.float32)
    inverse = lax.rsqrt(jnp.mean(widened * widened, axis=-1, keepdims=True) + norm_eps)
    seq_pos = lax.axis_index("seq") * tok_dev + jnp.arange(tok_dev, dtype=jnp.int32)
    positions = jnp.tile(seq_pos, micro_count)
    gain_piece = lax.all_gather(in_gain, "seq", axis=0, tiled=True)
    query_piece = lax.all_gather(w_query, "seq", axis=0, tiled=True)
    key_piece = lax.all_gather(w_key, "seq", axis=0, tiled=True)
    value_piece = lax.all_gather(w_value, "seq", axis=0, tiled=True)
    post_piece = lax.all_gather(post_gain, "seq", axis=0, tiled=True)
    final_piece = lax.all_gather(final_gain, "seq", axis=0, tiled=True)
    head_piece = lax.all_gather(value_head, "seq", axis=0, tiled=True)
    normed = (widened * inverse * gain_piece.astype(jnp.float32)).astype(jnp.bfloat16)
    query_acc = jnp.dot(normed, query_piece, preferred_element_type=jnp.float32)
    key_acc = jnp.dot(normed, key_piece, preferred_element_type=jnp.float32)
    value_acc = jnp.dot(normed, value_piece, preferred_element_type=jnp.float32)
    post_full = post_piece.astype(jnp.float32)
    final_full = final_piece.astype(jnp.float32)
    head_full = head_piece.astype(jnp.float32)
    folded = (query_acc, key_acc, value_acc, post_full, final_full, head_full)
    queries = folded[0].reshape(row_count, heads_here, GROUP, HD)
    queries = (rotate_pairs(rms_scale(queries, query_gain), positions) * query_scale).astype(
        jnp.bfloat16
    )
    keys_new = folded[1].reshape(row_count, heads_here, HD)
    keys_new = (
        rotate_pairs(rms_scale(keys_new, key_gain), positions)
        .astype(jnp.bfloat16)
        .reshape(row_count, kwidth)
    )
    vals_new = folded[2].astype(jnp.bfloat16)
    packed = jnp.concatenate([keys_new, vals_new], axis=1).reshape(micro_count, tok_dev, 2 * kwidth)
    window_rows = window_blocks(packed, tok_dev)
    key_pos = seq_pos[0] - WINDOW + jnp.arange(WINDOW + tok_dev, dtype=jnp.int32)
    mixed_list = []
    for micro_id in range(micro_count):
        block_queries = queries[micro_id * tok_dev : (micro_id + 1) * tok_dev]
        keys_all = window_rows[micro_id, :, :kwidth].reshape(-1, heads_here, HD)
        values_all = window_rows[micro_id, :, kwidth:].reshape(-1, heads_here, HD)
        mixed_list.append(
            window_attention(block_queries, keys_all, values_all, seq_pos, key_pos).reshape(
                tok_dev, qwidth
            )
        )
    mixed_all = jnp.concatenate(mixed_list, axis=0)
    branch = jnp.dot(
        mixed_all,
        lax.all_gather(w_out, "seq", axis=1, tiled=True),
        preferred_element_type=jnp.float32,
    )
    post_full, final_full, head_full = (folded[3], folded[4], folded[5])
    share_width = width // lax.axis_size("section")
    offset = lax.axis_index("section") * share_width
    share = lax.psum_scatter(branch, "section", scatter_dimension=1, tiled=True)
    branch_sq = lax.psum(jnp.sum(share * share, axis=1), "section")
    share_scale = lax.rsqrt(branch_sq / width + norm_eps)[:, None]
    post_share = lax.dynamic_slice_in_dim(post_full, offset, share_width, 0)
    updated = (
        lax.dynamic_slice_in_dim(widened, offset, share_width, 1) + share * share_scale * post_share
    ).astype(jnp.bfloat16)
    updated_wide = updated.astype(jnp.float32)
    residual_sq = lax.psum(jnp.sum(updated_wide * updated_wide, axis=1), "section")
    final_share = lax.dynamic_slice_in_dim(final_full, offset, share_width, 0)
    last_rows = (
        updated_wide * lax.rsqrt(residual_sq / width + norm_eps)[:, None] * final_share
    ).astype(jnp.bfloat16)
    head_share = lax.dynamic_slice_in_dim(head_full, offset, share_width, 0).astype(jnp.bfloat16)
    raw_values = lax.psum(
        jnp.dot(last_rows, head_share, preferred_element_type=jnp.float32), "section"
    )
    raw_values = raw_values.reshape(micro_count, tok_dev)
    token_values = jnp.where(seq_pos[None, :] < lengths[:, None], raw_values, 0.0)
    partial_value = jnp.sum(
        jnp.where(seq_pos[None, :] == reward_pos[:, None], token_values, 0.0), axis=1
    )
    reward = lax.psum(partial_value, "seq")
    return (token_values, reward)


def solution(mesh):
    placed = (
        P(None, "seq", None),
        P(),
        P(),
        P("seq"),
        P("seq", "section"),
        P("seq", "section"),
        P("seq", "section"),
        P(),
        P(),
        P("section", "seq"),
        P("seq"),
        P("seq"),
        P("seq"),
    )
    return jax.shard_map(
        local, mesh=mesh, in_specs=placed, out_specs=(P(None, "seq"), P()), check_vma=False
    )
```

profile of v0, /device:TPU:0, one launch (start us, length us, event | category | flops | bytes accessed | tf_op | source)
XLA Modules:
  0.0 331.5 jit_solution(10913897586998984354)
XLA Ops:
  15.5 39.5 %all-reduce.4 = (bf16[2688]{0:T(1024)(128)(2,1)S(1)}, bf16[2688]{0:T(1024)(128)(2,1)S(1)}, bf16[2688]{0:T(1024)(128)(2,1)S(1)}, bf16[2688]{0:T(1024)(128)(2,1)S(1)}) all-reduce(bf16[2688]{0:T(1024)(128)(2,1)S(1)} %dynamic-update-slice.3, bf16[2688]{0:T(1024)(128)(2,1)S(1)} %dynamic-update-slice, ...), channel_id=1, replica_groups=mesh['section'=4,'seq'=8] {'seq'}, use_global_device_ids=true, to_apply=%add.3 | all-reduce | flops 10752 | bytes 43008
  55.1 1.7 multiply_reduce_fusion
  56.8 1.7 copy.43
  58.4 2.9 multiply_convert_fusion.1
  61.7 2.6 copy.24
  64.3 2.4 multiply_reduce_fusion.3
  66.9 31.5 %all-gather.7.cloned.1.call-done = bf16[2688,256]{1,0:T(8,128)(2,1)} async-done(((bf16[336,256]{1,0:T(8,128)(2,1)}), bf16[2688,256]{1,0:T(8,128)(2,1)}) %all-gather.7.cloned.1.call-update) | async-done | bytes 1376272 | tf_op jit(solution)/shard_map/all_gather | solution.py:97
  98.4 2.4 fusion.15
  101.6 4.0 %collective-permute-start.1 = (bf16[2,128,512]{1,2,0:T(8,128)(2,1)S(1)}, bf16[2,128,512]{1,2,0:T(8,128)(2,1)S(1)}, u32[]{:S(2)}, u32[]{:S(2)}) collective-permute-start(bf16[2,128,512]{1,2,0:T(8,128)(2,1)S(1)} %pad_maximum_fusion), channel_id=1, source_target_pairs={{0,7},{8,15},{16,23},{24,31}} | collective-permute-start | bytes 786440 | tf_op jit(solution)/shard_map/ppermute | solution.py:19
  106.9 1.5 and_and_fusion
  111.0 2.4 collective-permute-start.5
  113.6 2.9 collective-permute-done.1
  117.8 9.9 %collective-permute-done.2 = bf16[2,128,512]{1,2,0:T(8,128)(2,1)S(1)} collective-permute-done((bf16[2,128,512]{1,2,0:T(8,128)(2,1)S(1)}, bf16[2,128,512]{1,2,0:T(8,128)(2,1)S(1)}, u32[]{:S(2)}, u32[]{:S(2)}) %collective-permute-start.2) | collective-permute-done | bytes 262176 | tf_op jit(solution)/shard_map/ppermute | solution.py:19
  127.7 1.5 collective-permute-start.7
  129.2 5.3 %collective-permute-done.3 = bf16[2,128,512]{1,2,0:T(8,128)(2,1)S(1)} collective-permute-done((bf16[2,128,512]{1,2,0:T(8,128)(2,1)S(1)}, bf16[2,128,512]{1,2,0:T(8,128)(2,1)S(1)}, u32[]{:S(2)}, u32[]{:S(2)}) %collective-permute-start.3) | collective-permute-done | bytes 262176 | tf_op jit(solution)/shard_map/ppermute | solution.py:19
  134.6 5.6 %collective-permute-done.4 = bf16[2,128,512]{1,2,0:T(8,128)(2,1)S(1)} collective-permute-done((bf16[2,128,512]{1,2,0:T(8,128)(2,1)S(1)}, bf16[2,128,512]{1,2,0:T(8,128)(2,1)S(1)}, u32[]{:S(2)}, u32[]{:S(2)}) %collective-permute-start.4) | collective-permute-done | bytes 262176 | tf_op jit(solution)/shard_map/ppermute | solution.py:19
  140.3 5.6 %collective-permute-done.5 = bf16[2,128,512]{1,2,0:T(8,128)(2,1)S(1)} collective-permute-done((bf16[2,128,512]{1,2,0:T(8,128)(2,1)S(1)}, bf16[2,128,512]{1,2,0:T(8,128)(2,1)S(1)}, u32[]{:S(2)}, u32[]{:S(2)}) %collective-permute-start.5) | collective-permute-done | bytes 262176 | tf_op jit(solution)/shard_map/ppermute | solution.py:19
  145.9 3.4 %collective-permute-done.6 = bf16[2,128,512]{1,2,0:T(8,128)(2,1)S(1)} collective-permute-done((bf16[2,128,512]{1,2,0:T(8,128)(2,1)S(1)}, bf16[2,128,512]{1,2,0:T(8,128)(2,1)S(1)}, u32[]{:S(2)}, u32[]{:S(2)}) %collective-permute-start.6) | collective-permute-done | bytes 262176 | tf_op jit(solution)/shard_map/ppermute | solution.py:19
  150.8 27.7 %all-gather.9.cloned.1.call-done = bf16[2688,512]{1,0:T(8,128)(2,1)} async-done(((bf16[336,512]{1,0:T(8,128)(2,1)}), bf16[2688,512]{1,0:T(8,128)(2,1)}) %all-gather.9.cloned.1.call-update) | async-done | bytes 2752528 | tf_op jit(solution)/shard_map/all_gather | solution.py:95
  178.5 4.5 %copy.27 = bf16[512,2688]{1,0:T(8,128)(2,1)} copy(bf16[512,2688]{0,1:T(8,128)(2,1)} %bitcast.94) | data formatting | bytes 5505024 | tf_op jit(solution)/shard_map/dot_general | solution.py:102
  183.0 3.2 multiply_reduce_fusion.2
  187.1 2.1 fusion.64
  189.2 1.8 fusion.61
  191.1 3.2 fusion.14
  194.3 3.1 fusion.13
  197.3 46.1 %all-gather.11.cloned.1.call-done = bf16[512,2688]{0,1:T(8,128)(2,1)} async-done(((bf16[512,336]{0,1:T(8,128)(2,1)}), bf16[512,2688]{0,1:T(8,128)(2,1)}) %all-gather.11.cloned.1.call-update) | async-done | bytes 2752528 | tf_op jit(solution)/shard_map/all_gather | solution.py:136
  243.4 4.3 %fusion.24 = f32[256,2688]{0,1:T(8,128)} fusion(bf16[512,2688]{0,1:T(8,128)(2,1)} %all-gather.11.cloned.1.call-done, bf16[128,512]{0,1:T(8,128)(2,1)} %bitcast.108, bf16[128,512]{0,1:T(8,128)(2,1)} %bitcast.107), kind=kOutput, calls=%fused_computation.39 | convolution fusion | flops 705167360 | bytes 5767168 | tf_op jit(solution)/shard_map/dot_general | solution.py:134
  248.0 33.8 %reduce-scatter.2.cloned.1.call-done = f32[256,672]{0,1:T(8,128)} async-done(((f32[256,2688]{0,1:T(8,128)}), f32[256,672]{0,1:T(8,128)}) %reduce-scatter.2.cloned.1.call-update) | async-done | bytes 688144 | tf_op jit(solution)/shard_map/reduce_scatter | solution.py:142
  283.0 5.8 %psum.28 = f32[256]{0:T(256)S(1)} all-reduce(f32[256]{0:T(256)S(1)} %multiply_reduce_fusion.1), channel_id=1, replica_groups=mesh['section'=4,'seq'=8] {'section'}, use_global_device_ids=true, to_apply=%region_9.10 | all-reduce | flops 256 | bytes 2048 | tf_op jit(solution)/shard_map/psum | solution.py:143
  290.1 5.7 %psum.29 = f32[256]{0:T(256)S(1)} all-reduce(f32[256]{0:T(256)S(1)} %get-tuple-element.8), channel_id=1, replica_groups=mesh['section'=4,'seq'=8] {'section'}, use_global_device_ids=true, to_apply=%region_11.12 | all-reduce | flops 256 | bytes 2048 | tf_op jit(solution)/shard_map/psum | solution.py:150
  296.0 6.3 %psum.30 = f32[2,128]{1,0:T(2,128)S(1)} all-reduce(f32[2,128]{1,0:T(2,128)S(1)} %bitcast.110), channel_id=1, replica_groups=mesh['section'=4,'seq'=8] {'section'}, use_global_device_ids=true, to_apply=%region_12.13 | all-reduce | flops 256 | bytes 2048 | tf_op jit(solution)/shard_map/psum | solution.py:156
  303.1 21.9 %psum.31 = f32[2]{0:T(128)} all-reduce(f32[2]{0:T(128)S(1)} %get-tuple-element.6), channel_id=1, replica_groups=mesh['section'=4,'seq'=8] {'seq'}, use_global_device_ids=true, to_apply=%region_14.15 | all-reduce | flops 2 | bytes 16 | tf_op jit(solution)/shard_map/psum | solution.py:164
  (78 shorter events, 20.7 us)
Async XLA Ops:
  7.2 54.5 %all-gather.5.cloned.1.call-start = ((), (), s32[]{:S(2)}) async-start(), calls=%async_computation.1 | async-start | bytes 1548288 | tf_op jit(solution)/shard_map/all_gather | solution.py:96
  7.9 90.5 %all-gather.7.cloned.1.call-start = ((), (), s32[]{:S(2)}) async-start(), calls=%async_computation.2 | async-start | bytes 1548288 | tf_op jit(solution)/shard_map/all_gather | solution.py:97
  8.6 169.8 %all-gather.9.cloned.1.call-start = ((), (), s32[]{:S(2)}) async-start(), calls=%async_computation.3 | async-start | bytes 3096576 | tf_op jit(solution)/shard_map/all_gather | solution.py:95
  9.4 234.0 %all-gather.11.cloned.1.call-start = ((), (), s32[]{:S(2)}) async-start(), calls=%async_computation.4 | async-start | bytes 3096576 | tf_op jit(solution)/shard_map/all_gather | solution.py:136
  10.0 271.8 %reduce-scatter.2.cloned.1.call-start = ((), (), s32[]{:S(2)}) async-start(), calls=%async_computation.5 | async-start | bytes 3440640 | tf_op jit(solution)/shard_map/reduce_scatter | solution.py:142
  61.7 5.0 %copy-start.1 = (f32[128]{0:T(128)S(1)}, f32[128]{0:T(128)}, u32[]{:S(2)}) copy-start(f32[128]{0:T(128)} %param.21) | copy-start | bytes 1540
  100.9 10.1 %collective-permute-start = (bf16[2,128,512]{1,2,0:T(8,128)(2,1)S(1)}, bf16[2,128,512]{1,2,0:T(8,128)(2,1)S(1)}, u32[]{:S(2)}, u32[]{:S(2)}) collective-permute-start(bf16[2,128,512]{1,2,0:T(8,128)(2,1)S(1)} %pad_maximum_fusion), channel_id=1, source_target_pairs={} | collective-permute-start | bytes 786440 | tf_op jit(solution)/shard_map/ppermute | solution.py:19
  101.6 14.9 %collective-permute-start.1 = (bf16[2,128,512]{1,2,0:T(8,128)(2,1)S(1)}, bf16[2,128,512]{1,2,0:T(8,128)(2,1)S(1)}, u32[]{:S(2)}, u32[]{:S(2)}) collective-permute-start(bf16[2,128,512]{1,2,0:T(8,128)(2,1)S(1)} %pad_maximum_fusion), channel_id=1, source_target_pairs={{0,7},{8,15},{16,23},{24,31}} | collective-permute-start | bytes 786440 | tf_op jit(solution)/shard_map/ppermute | solution.py:19
  105.6 22.1 %collective-permute-start.2 = (bf16[2,128,512]{1,2,0:T(8,128)(2,1)S(1)}, bf16[2,128,512]{1,2,0:T(8,128)(2,1)S(1)}, u32[]{:S(2)}, u32[]{:S(2)}) collective-permute-start(bf16[2,128,512]{1,2,0:T(8,128)(2,1)S(1)} %pad_maximum_fusion), channel_id=1, source_target_pairs={{0,6},{1,7},{8,14},{9,15},{16,22},{17,23},{24,30},{25,31}} | collective-permute-start | bytes 786440 | tf_op jit(solution)/shard_map/ppermute | solution.py:19
  108.4 26.2 %collective-permute-start.3 = (bf16[2,128,512]{1,2,0:T(8,128)(2,1)S(1)}, bf16[2,128,512]{1,2,0:T(8,128)(2,1)S(1)}, u32[]{:S(2)}, u32[]{:S(2)}) collective-permute-start(bf16[2,128,512]{1,2,0:T(8,128)(2,1)S(1)} %pad_maximum_fusion), channel_id=1, source_target_pairs={{0,5},{1,6},{2,7},{8,13},{9,14},{10,15},{16,21},{17,22},{18,23},{2... | collective-permute-start | bytes 786440 | tf_op jit(solution)/shard_map/ppermute | solution.py:19
  109.7 30.5 %collective-permute-start.4 = (bf16[2,128,512]{1,2,0:T(8,128)(2,1)S(1)}, bf16[2,128,512]{1,2,0:T(8,128)(2,1)S(1)}, u32[]{:S(2)}, u32[]{:S(2)}) collective-permute-start(bf16[2,128,512]{1,2,0:T(8,128)(2,1)S(1)} %pad_maximum_fusion), channel_id=1, source_target_pairs={{0,4},{1,5},{2,6},{3,7},{8,12},{9,13},{10,14},{11,15},{16,20},{17,... | collective-permute-start | bytes 786440 | tf_op jit(solution)/shard_map/ppermute | solution.py:19
  111.0 34.8 %collective-permute-start.5 = (bf16[2,128,512]{1,2,0:T(8,128)(2,1)S(1)}, bf16[2,128,512]{1,2,0:T(8,128)(2,1)S(1)}, u32[]{:S(2)}, u32[]{:S(2)}) collective-permute-start(bf16[2,128,512]{1,2,0:T(8,128)(2,1)S(1)} %pad_maximum_fusion), channel_id=1, source_target_pairs={{0,3},{1,4},{2,5},{3,6},{4,7},{8,11},{9,12},{10,13},{11,14},{12,15... | collective-permute-start | bytes 786440 | tf_op jit(solution)/shard_map/ppermute | solution.py:19
  116.5 32.9 %collective-permute-start.6 = (bf16[2,128,512]{1,2,0:T(8,128)(2,1)S(1)}, bf16[2,128,512]{1,2,0:T(8,128)(2,1)S(1)}, u32[]{:S(2)}, u32[]{:S(2)}) collective-permute-start(bf16[2,128,512]{1,2,0:T(8,128)(2,1)S(1)} %pad_maximum_fusion), channel_id=1, source_target_pairs={{0,2},{1,3},{2,4},{3,5},{4,6},{5,7},{8,10},{9,11},{10,12},{11,13},... | collective-permute-start | bytes 786440 | tf_op jit(solution)/shard_map/ppermute | solution.py:19
  127.7 21.7 %collective-permute-start.7 = (bf16[2,128,512]{1,2,0:T(8,128)(2,1)S(1)}, bf16[2,128,512]{1,2,0:T(8,128)(2,1)S(1)}, u32[]{:S(2)}, u32[]{:S(2)}) collective-permute-start(bf16[2,128,512]{1,2,0:T(8,128)(2,1)S(1)} %pad_maximum_fusion), channel_id=1, source_target_pairs={{0,1},{1,2},{2,3},{3,4},{4,5},{5,6},{6,7},{8,9},{9,10},{10,11},{11... | collective-permute-start | bytes 786440 | tf_op jit(solution)/shard_map/ppermute | solution.py:19
  183.0 3.2 copy-start.2
  186.4 2.9 copy-start
  247.7 54.6 %copy-start.3 = (s32[2]{0:T(128)S(1)}, s32[2]{0:T(128)}, u32[]{:S(2)}) copy-start(s32[2]{0:T(128)} %param.15) | copy-start | bytes 28
  247.7 54.6 %copy-start.4 = (s32[2]{0:T(128)S(1)}, s32[2]{0:T(128)}, u32[]{:S(2)}) copy-start(s32[2]{0:T(128)} %param.14) | copy-start | bytes 28
Sparse Core Ops, SparseCore 0:
  10.2 45.0 all-gather.4
  57.4 40.9 all-gather.6
  100.6 77.8 all-gather.8
  180.5 62.8 all-gather.10
  247.9 33.8 reduce-scatter.1
where the time goes:
time: 332 us; the launch traced here: 331 us
  waiting for transfers between devices  174 us (52%)
  blocking collectives  79.1 us (24%)
  matrix products  22.7 us (7%)
  local copies, waits for them, and re-layouts  15.4 us (5%)
  between operations  14.8 us (4%)
  starting transfers between devices  14 us (4%)
  other arithmetic  11.1 us (3%)
    all_gather x1, waiting for transfers between devices, local(): lax.all_gather(w_out, 'seq', axis=1, tiled=True)  46.1 us
    unnamed x1, blocking collectives  39.5 us
    reduce_scatter x1, waiting for transfers between devices, local(): share = lax.psum_scatter(branch, 'section', scatter_dimension=1, tiled=True)  33.8 us
    ppermute x8, waiting for transfers between devices, passed_along(): return lax.ppermute(array, axis, pairs)  32.7 us
    all_gather x1, waiting for transfers between devices, local(): value_piece = lax.all_gather(w_value, 'seq', axis=0, tiled=True)  31.5 us
    all_gather x1, waiting for transfers between devices, local(): query_piece = lax.all_gather(w_query, 'seq', axis=0, tiled=True)  27.7 us
    psum x1, blocking collectives, local(): reward = lax.psum(partial_value, 'seq')  21.9 us
    ppermute x8, starting transfers between devices, passed_along(): return lax.ppermute(array, axis, pairs)  13.8 us
  transfers between devices with their start and end apart: 13, of which 10 were waited for; matrix products, arithmetic and copies ran while one was open for 12% of the time, Pallas kernels for 0%

commit v1 on v0

--- a/solution.py
+++ b/solution.py
@@ -1,6 +1,9 @@
 import jax
 import jax.numpy as jnp
+import numpy as np
 from jax import lax
+from jax.experimental import pallas as pl
+from jax.experimental.pallas import tpu as pltpu
 from jax.sharding import PartitionSpec as P
 
 HD = 128
@@ -65,6 +68,383 @@
         "hgqk,khd->qhgd", attn_weights, values_all, preferred_element_type=jnp.float32
     )
     return mixed_heads.astype(jnp.bfloat16)
+
+
+MESH = pl.DeviceIdType.MESH
+
+
+def kernel(
+    hid, wp, wo, gp, hg, cos_t, sin_t, out,
+    xb, wb, wob, gb, gfull, qs, ks, vs, ms, mb, bp, bs, br, hs, sr, rs, rr,
+    ws1, ws2, ws3, w_r, xs1, xs2, xs3, xs4, x_r, os_, o_r, gs, g_r, mss, m_r,
+    b_s, b_r, ss, s_r, rss, r_r,
+):
+    sec = lax.axis_index("section")
+    seq = lax.axis_index("seq")
+    x, g = sec // 2, sec % 2
+    z, y = seq // 2, seq % 2
+    tok = hid.shape[1]
+    width = hid.shape[2]
+    n_z = 4
+    n_s = 8
+    rows = wp.shape[1]
+    part = tok // 4
+    tokens = n_s * tok
+    half = tokens // 2
+    quarter = tokens // 4
+    xsec = (sec + 2) % 4
+    csec = x * 2 + (1 - g)
+
+    def remote(src, dst, s_sem, r_sem, c2, s2):
+        return pltpu.make_async_remote_copy(
+            src_ref=src, dst_ref=dst, send_sem=s_sem, recv_sem=r_sem,
+            device_id=(c2, s2), device_id_type=MESH,
+        )
+
+    def arrived(dst, r_sem):
+        pltpu.make_async_copy(dst, dst, r_sem).wait()
+
+    def w_at(s2):
+        return wb.at[pl.ds(pl.multiple_of(s2 * rows, 16), rows), :]
+
+    sends = []
+    for k in range(1, n_s):
+        s2 = (seq + k) % n_s
+        cp = remote(gp, gb.at[seq], gs.at[k], g_r.at[seq], sec, s2)
+        cp.start()
+        sends.append(cp)
+    local_g = pltpu.make_async_copy(gp, gb.at[seq], g_r.at[seq])
+    local_g.start()
+
+    def x_part(m):
+        return hid.at[m, pl.ds(pl.multiple_of(sec * part, 16), part), :]
+
+    def w_send(h):
+        zd = 2 * g + h
+        cp = remote(wp.at[h], w_at(seq), ws1.at[h], w_r.at[seq], sec, 2 * zd + y)
+
+        @pl.when(zd != z)
+        def _():
+            cp.start()
+
+        @pl.when(zd == z)
+        def _():
+            pltpu.make_async_copy(wp.at[h], w_at(seq), w_r.at[seq]).start()
+
+        return zd != z, cp
+
+    pltpu.make_async_copy(x_part(y), xb.at[seq, sec], x_r.at[seq, sec]).start()
+    cp = remote(x_part(1 - y), xb.at[seq, sec], xs1.at[1], x_r.at[seq, sec], sec, 2 * z + 1 - y)
+    cp.start()
+    sends.append(cp)
+    cond_sends = [w_send(0), w_send(1)]
+    for k in range(1, n_z):
+        zd = (z + k) % n_z
+        for j in range(2):
+            m = (y + j) % 2
+            cp = remote(
+                x_part(m), xb.at[seq, sec], xs1.at[2 * k + j], x_r.at[seq, sec], sec, 2 * zd + m
+            )
+            cp.start()
+            sends.append(cp)
+
+    w_home = g == z // 2
+    for k in range(n_z):
+        z2 = (z - k + n_z) % n_z
+        s2 = 2 * z2 + y
+        yf = remote(w_at(s2), w_at(s2), ws2.at[k], w_r.at[s2], sec, 2 * z + 1 - y)
+        cf = remote(w_at(s2), w_at(s2), ws3.at[k], w_r.at[s2], csec, seq)
+
+        @pl.when(w_home)
+        def _():
+            arrived(w_at(s2), w_r.at[s2])
+            yf.start()
+            cf.start()
+
+        cond_sends += [(w_home, yf), (w_home, cf)]
+        for j in range(2):
+            s2 = 2 * z2 + (y + j) % 2
+            arrived(xb.at[s2, sec], x_r.at[s2, sec])
+            i = 2 * k + j
+            xf = remote(
+                xb.at[s2, sec], xb.at[s2, sec], xs2.at[i], x_r.at[s2, sec], xsec, seq
+            )
+            xf.start()
+            cx = remote(
+                xb.at[s2, sec], xb.at[s2, sec], xs3.at[i], x_r.at[s2, sec], csec, seq
+            )
+            cx.start()
+            sends += [xf, cx]
+    own_o = wob.at[y, pl.ds(pl.multiple_of(g * 512, 512), 512), :]
+    i = 0
+    for dy in range(2):
+        for dg in range(2):
+            if dy == 0 and dg == 0:
+                pltpu.make_async_copy(wo, own_o, o_r.at[2 * y + g]).start()
+            else:
+                cp = remote(
+                    wo, own_o, os_.at[i], o_r.at[2 * y + g],
+                    x * 2 + (g + dg) % 2, 2 * z + (y + dy) % 2,
+                )
+                cp.start()
+                sends.append(cp)
+            i += 1
+    for k in range(n_z):
+        z2 = (z - k + n_z) % n_z
+        s2 = 2 * z2 + 1 - y
+        cf = remote(w_at(s2), w_at(s2), ws3.at[n_z + k], w_r.at[s2], csec, seq)
+
+        @pl.when(w_home)
+        def _():
+            arrived(w_at(s2), w_r.at[s2])
+            cf.start()
+
+        cond_sends.append((w_home, cf))
+
+    @pl.when(jnp.logical_not(w_home))
+    def _():
+        for s2 in range(n_s):
+            arrived(w_at(s2), w_r.at[s2])
+
+    for s2 in range(n_s):
+        arrived(gb.at[s2], g_r.at[s2])
+        gfull[:, s2 * rows : (s2 + 1) * rows] = gb[s2]
+    for k in range(n_z):
+        for j in range(2):
+            s2 = 2 * ((z - k + n_z) % n_z) + (y + j) % 2
+            arrived(xb.at[s2, xsec], x_r.at[s2, xsec])
+            cp = remote(
+                xb.at[s2, xsec], xb.at[s2, xsec], xs4.at[2 * k + j], x_r.at[s2, xsec], csec, seq
+            )
+            cp.start()
+            sends.append(cp)
+
+    def project(k, carry):
+        s2 = 2 * ((z - k // 2 + n_z) % n_z) + (y + k % 2) % 2
+        arrived(xb.at[s2, csec], x_r.at[s2, csec])
+        c3 = (csec + 2) % 4
+        arrived(xb.at[s2, c3], x_r.at[s2, c3])
+        wide = xb[s2].reshape(tok, width).astype(jnp.float32)
+        inv = lax.rsqrt(jnp.mean(wide * wide, axis=-1, keepdims=True) + norm_eps)
+        normed = (wide * inv * gfull[0:1, :]).astype(jnp.bfloat16)
+        acc = jnp.dot(normed, wb[...], preferred_element_type=jnp.float32)
+        here = pl.ds(pl.multiple_of(s2 * tok, tok), tok)
+        cos_b = cos_t[here, :]
+        sin_b = sin_t[here, :]
+
+        def turned(u, gain):
+            u = u * lax.rsqrt(jnp.mean(u * u, axis=-1, keepdims=True) + norm_eps) * gain
+            return u * cos_b + pltpu.roll(u, HD // 2, 1) * sin_b
+
+        q = jnp.where(g == 0, acc[:, :HD], acc[:, HD : 2 * HD])
+        qs[here, :] = (turned(q, hg[0:1, :]) * query_scale).astype(jnp.bfloat16)
+        ks[here, :] = turned(acc[:, 2 * HD : 3 * HD], hg[1:2, :]).astype(jnp.bfloat16)
+        vs[here, :] = acc[:, 3 * HD :].astype(jnp.bfloat16)
+        return carry
+
+    lax.fori_loop(0, n_s, project, 0)
+
+    head_id = 2 * z + g
+
+    def m_slot(h):
+        return mb.at[h]
+
+    blk = tokens // 4
+    for qb in range(4):
+        span = (qb + 1) * blk
+        q = qs[qb * blk : span, :]
+        sc = lax.dot_general(
+            q, ks[:span, :], (((1,), (1,)), ((), ())), preferred_element_type=jnp.float32
+        )
+        qi = lax.broadcasted_iota(jnp.int32, (blk, span), 0) + qb * blk
+        ki = lax.broadcasted_iota(jnp.int32, (blk, span), 1)
+        sc = jnp.where((ki <= qi) & (ki > qi - WINDOW), sc, -1e30)
+        ex = jnp.exp(sc - jnp.max(sc, axis=-1, keepdims=True))
+        pr = (ex / jnp.sum(ex, axis=-1, keepdims=True)).astype(jnp.bfloat16)
+        ms[qb * blk : span, :] = jnp.dot(
+            pr, vs[:span, :], preferred_element_type=jnp.float32
+        ).astype(jnp.bfloat16)
+        if qb % 2 == 1:
+            gd = qb // 2
+            src = ms.at[pl.ds(gd * half, half), :]
+            for k in range(1, n_z):
+                zd = (z + k) % n_z
+                cp = remote(
+                    src, m_slot(head_id), mss.at[gd, k], m_r.at[head_id], 2 * x + gd, 2 * zd + y
+                )
+                cp.start()
+                sends.append(cp)
+            cp = remote(src, m_slot(head_id), mss.at[gd, 0], m_r.at[head_id], csec, seq)
+
+            @pl.when(g != gd)
+            def _():
+                cp.start()
+
+            @pl.when(g == gd)
+            def _():
+                pltpu.make_async_copy(src, m_slot(head_id), m_r.at[head_id]).start()
+
+            cond_sends.append((g != gd, cp))
+
+    first = 4 * g + 2 * x
+    for zz in range(n_z):
+
+        @pl.when(z == zz)
+        def _():
+            for b2 in range(2):
+                blockv = xb[first + b2].reshape(tok, width)
+                for yc in range(2):
+                    lo = (2 * zz + yc) * rows
+                    hs[yc, b2 * tok : (b2 + 1) * tok, :] = blockv[:, lo : lo + rows].astype(
+                        jnp.float32
+                    )
+
+    for i in range(4):
+        o_here = wob.at[i // 2, pl.ds((i % 2) * 512, 512), :]
+        arrived(o_here, o_r.at[i])
+    for h in range(n_s):
+        arrived(m_slot(h), m_r.at[h])
+    mixed = jnp.concatenate([mb[h] for h in range(n_s)], axis=1)
+    for yc in range(2):
+        bp[yc] = jnp.dot(mixed, wob[yc], preferred_element_type=jnp.float32)
+    away = pl.ds(pl.multiple_of((1 - x) * quarter, quarter), quarter)
+    home = pl.ds(pl.multiple_of(x * quarter, quarter), quarter)
+    for yc in range(2):
+        bs[yc] = bp[yc, away, :].astype(jnp.bfloat16)
+    cp = remote(bs, br, b_s, b_r, xsec, seq)
+    cp.start()
+    sends.append(cp)
+    arrived(br, b_r)
+    cols = [jnp.zeros((quarter, 1), jnp.float32)] * 6
+    for yc in range(2):
+        b = bp[yc, home, :] + br[yc].astype(jnp.float32)
+        h = hs[yc]
+        gains = gb[2 * z + yc]
+        post = gains[1:2, :]
+        tip = gains[2:3, :] * gains[3:4, :]
+        pb = post * b
+        terms = (b * b, h * pb, pb * pb, pb * tip, h * h, h * tip)
+        cols = [c0 + jnp.sum(t, axis=-1, keepdims=True) for c0, t in zip(cols, terms)]
+    lane = lax.broadcasted_iota(jnp.int32, (quarter, 128), 1)
+    table = jnp.zeros((quarter, 128), jnp.float32)
+    for i, c0 in enumerate(cols):
+        table = jnp.where(lane == i, c0, table)
+    sr[z] = table.T[:8, :]
+    for k in range(1, n_z):
+        zd = (z + k) % n_z
+        cp = remote(sr.at[z], sr.at[z], ss.at[k], s_r.at[z], sec, 2 * zd + y)
+        cp.start()
+        sends.append(cp)
+    for k in range(1, n_z):
+        z2 = (z + k) % n_z
+        arrived(sr.at[z2], s_r.at[z2])
+    st = sr[0] + sr[1] + sr[2] + sr[3]
+    r1 = lax.rsqrt(st[0:1] / width + norm_eps)
+    res_sq = st[4:5] + 2.0 * r1 * st[1:2] + r1 * r1 * st[2:3]
+    r2 = lax.rsqrt(res_sq / width + norm_eps)
+    raw = r2 * (st[5:6] + r1 * st[3:4])
+    spot = 4 * y + 2 * g + x
+    rr[spot] = jnp.broadcast_to(raw, (8, quarter))
+    for i in range(1, 8):
+        c2 = (sec + i % 4) % 4
+        y2 = (y + i // 4) % 2
+        cp = remote(rr.at[spot], rr.at[spot], rss.at[i], r_r.at[spot], c2, 2 * z + y2)
+        cp.start()
+        sends.append(cp)
+    for i in range(1, 8):
+        c2 = (sec + i % 4) % 4
+        y2 = (y + i // 4) % 2
+        sp2 = 4 * y2 + 2 * (c2 % 2) + c2 // 2
+        arrived(rr.at[sp2], r_r.at[sp2])
+    for i in range(8):
+        out[i : i + 1, :] = rr[i, 0:1, :]
+    for cp in sends:
+        cp.wait_send()
+    for cond, cp in cond_sends:
+
+        @pl.when(cond)
+        def _():
+            cp.wait_send()
+
+
+def rope_tables(tokens):
+    half_width = HD // 2
+    frequency = rope_base ** (-np.arange(half_width, dtype=np.float32) * 2.0 / HD)
+    angles = np.arange(tokens, dtype=np.float32)[:, None] * frequency.astype(np.float32)[None, :]
+    cosine, sine = np.cos(angles), np.sin(angles)
+    return (
+        np.concatenate([cosine, cosine], axis=1).astype(np.float32),
+        np.concatenate([-sine, sine], axis=1).astype(np.float32),
+    )
+
+
+def fused(
+    hidden, lengths, reward_pos, in_gain, w_query, w_key, w_value, query_gain, key_gain,
+    w_out, post_gain, final_gain, value_head,
+):
+    micro_count, tok, width = hidden.shape
+    rows = w_query.shape[0]
+    tokens = tok * lax.axis_size("seq")
+    quarter = tokens // 4
+    wp = jnp.concatenate(
+        [
+            w_query.reshape(rows, 2, GROUP * HD),
+            w_key.reshape(rows, 2, HD),
+            w_value.reshape(rows, 2, HD),
+        ],
+        axis=2,
+    ).transpose(1, 0, 2)
+    gp = jnp.stack([in_gain, post_gain, final_gain, value_head] * 2).astype(jnp.float32)
+    hg = jnp.stack([query_gain, key_gain] * 4)
+    cos_t, sin_t = rope_tables(tokens)
+    bf, f32 = jnp.bfloat16, jnp.float32
+    V = pltpu.VMEM
+    dma = pltpu.SemaphoreType.DMA
+    raw = pl.pallas_call(
+        kernel,
+        out_shape=jax.ShapeDtypeStruct((8, quarter), f32),
+        in_specs=[pl.BlockSpec(memory_space=pltpu.VMEM)] * 7,
+        out_specs=pl.BlockSpec(memory_space=pltpu.VMEM),
+        scratch_shapes=[
+            V((8, 4, tok // 4, width), bf), V((width, 512), bf), V((2, 1024, rows), bf),
+            V((8, 8, rows), f32), V((8, width), f32),
+            V((tokens, HD), bf), V((tokens, HD), bf), V((tokens, HD), bf), V((tokens, HD), bf),
+            V((8, tokens // 2, HD), bf), V((2, tokens // 2, rows), f32),
+            V((2, quarter, rows), bf), V((2, quarter, rows), bf), V((2, quarter, rows), f32),
+            V((4, 8, quarter), f32), V((8, 128), f32), V((8, 8, quarter), f32),
+            dma((2,)), dma((4,)), dma((8,)), dma((8,)),
+            dma((8,)), dma((8,)), dma((8,)), dma((8,)), dma((8, 4)),
+            dma((4,)), dma((4,)), dma((8,)), dma((8,)), dma((2, 4)), dma((8,)),
+            dma, dma, dma((4,)), dma((4,)), dma((8,)), dma((8,)),
+        ],
+        compiler_params=pltpu.CompilerParams(
+            has_side_effects=True, vmem_limit_bytes=60 * 1024 * 1024
+        ),
+        name="whole_layer",
+    )(hidden, wp, w_out, gp, hg, cos_t, sin_t)
+    raw = raw.reshape(micro_count, tokens)
+    pos = jnp.arange(tokens, dtype=jnp.int32)[None, :]
+    full = jnp.where(pos < lengths[:, None], raw, 0.0)
+    reward = jnp.sum(jnp.where(pos == reward_pos[:, None], full, 0.0), axis=1)
+    mine = lax.dynamic_slice_in_dim(full, lax.axis_index("seq") * tok, tok, 1)
+    return (mine, reward)
+
+
+def choose(hidden, lengths, reward_pos, in_gain, w_query, w_key, w_value, query_gain, *rest):
+    sections, places = lax.axis_size("section"), lax.axis_size("seq")
+    fits = (
+        sections == 4
+        and places == 8
+        and hidden.shape[0] == 2
+        and hidden.shape[1] * places <= WINDOW
+        and hidden.shape[1] % 128 == 0
+        and w_key.shape[1] == 2 * HD
+        and w_query.shape[0] % 16 == 0
+    )
+    body = fused if fits else local
+    return body(
+        hidden, lengths, reward_pos, in_gain, w_query, w_key, w_value, query_gain, *rest
+    )
 
 
 def local(
@@ -182,5 +562,5 @@
         P("seq"),
     )
     return jax.shard_map(
-        local, mesh=mesh, in_specs=placed, out_specs=(P(None, "seq"), P()), check_vma=False
-    )
+        choose, mesh=mesh, in_specs=placed, out_specs=(P(None, "seq"), P()), check_vma=False
+    )

time: 332 us -> 129 us (0.39)
  waiting for transfers between devices: 174 us -> 0 us
  Pallas kernels: 0 us -> 119 us
  blocking collectives: 79.1 us -> 0 us
  matrix products: 22.7 us -> 0 us
  between operations: 14.8 us -> 0.76 us
  starting transfers between devices: 14 us -> 0 us
  local copies, waits for them, and re-layouts: 15.4 us -> 5.66 us
  other arithmetic: 11.1 us -> 3.67 us
    pallas_call x0 -> x1, Pallas kernels: none -> 119 us  [fused(): pl.pallas_call(kernel, out_shape=jax.ShapeDtypeStruct((8, quarter), f32),...]
    all_gather x4 -> x0, waiting for transfers between devices: 105 us -> none  [the longest x1 46.1 us: local(): lax.all_gather(w_out, 'seq', axis=1, tiled=True)]
    psum x4 -> x0, blocking collectives: 39.6 us -> none  [the longest x1 21.9 us: local(): reward = lax.psum(partial_value, 'seq')]
    unnamed x1 -> x0, blocking collectives: 39.5 us -> none
    reduce_scatter x1 -> x0, waiting for transfers between devices: 33.8 us -> none  [local(): share = lax.psum_scatter(branch, 'section', scatter_dimension=1, tiled=True)]
    ppermute x8 -> x0, waiting for transfers between devices: 32.7 us -> none  [passed_along(): return lax.ppermute(array, axis, pairs)]
    dot_general x7 -> x0, matrix products: 18.7 us -> none  [the longest x2 6.26 us: window_attention(): jnp.einsum('hgqk,khd->qhgd', attn_weights, values_all, preferred_element_...]
    ppermute x8 -> x0, starting transfers between devices: 13.8 us -> none  [passed_along(): return lax.ppermute(array, axis, pairs)]
  transfers between devices with their start and end apart: 13 -> 0, of which waited for: 10 -> 0; matrix products, arithmetic and copies ran while one was open for 12% -> 0% of each run, Pallas kernels for 0% -> 0%
where the time goes in v1:
time: 129 us
  Pallas kernels  119 us (92%)
  local copies, waits for them, and re-layouts  5.66 us (4%)
  other arithmetic  3.67 us (3%)
    pallas_call x1, Pallas kernels, fused(): pl.pallas_call(kernel, out_shape=jax.ShapeDtypeStruct((8, quarter), f32),...  119 us

profile of v1, /device:TPU:0, one launch (start us, length us, event | category | flops | bytes accessed | tf_op | source)
XLA Modules:
  0.0 128.7 jit_solution(18107178825042011858)
XLA Ops:
  0.6 0.0 copy-start
  0.6 0.0 copy-start.1
  0.7 0.9 copy-done
  1.6 1.0 copy_bitcast_fusion.1
  2.5 0.0 copy-start.4
  2.5 0.0 copy-start.5
  2.6 0.0 copy-start.6
  2.6 0.0 copy-start.7
  2.6 0.0 copy-start.2
  2.6 0.0 copy-start.3
  2.6 1.0 copy.28
  3.6 0.9 maximum_bitcast_fusion.wp
  4.6 0.0 copy-done.1
  4.6 0.9 copy.21.wo
  5.5 0.0 copy-done.4
  5.5 0.0 copy-done.5
  5.5 0.0 copy-done.6
  5.5 0.0 copy-done.7
  5.6 0.6 convert_element_type.3.gp
  6.2 0.0 copy-done.2
  6.2 0.0 copy-done.3
  6.2 0.6 stack.41.hg
  6.8 118.6 %whole_layer.1 = f32[8,256]{1,0:T(8,128)} custom-call(bf16[2,128,2688]{2,1,0:T(8,128)(2,1)} %hid.1, bf16[2,336,512]{2,1,0:T(8,128)(2,1)} %maximum_bitcast_fusion.wp, bf16[512,336]{1,0:T(8,128)(2,1)} %copy.21.wo, f32[8,336]{1,0:T(8,128)} %convert_element_type.3.gp, f32[8,128]{1,0:T(8,128)} %stack.41.hg, f32[1024,128]{1,0:T(8,128)} %constant.19.clone.cos_t, ...), custom_call_target="tpu_custom_call" | custom-call | tf_op jit(solution)/shard_map/whole_layer/pallas_call | solution.py:403
  125.4 0.7 reshape.28
  126.1 0.6 compare_select_fusion
  126.7 0.1 lt.52
  126.8 0.1 lt.53
  126.9 0.1 eq.16
  127.0 0.1 eq.17
  127.1 0.9 select_reduce_fusion
  127.9 0.1 reduce_sum.14
  128.0 0.6 reduce_sum.18
  (12 shorter events, 0.1 us)
Async XLA Ops:
  0.6 0.9 copy-start
  0.6 3.9 %copy-start.1 = (bf16[512,336]{0,1:T(8,128)(2,1)S(1)}, bf16[512,336]{0,1:T(8,128)(2,1)}, u32[]{:S(2)}) copy-start(bf16[512,336]{0,1:T(8,128)(2,1)} %param.24) | copy-start | bytes 1032196
  2.5 2.9 %copy-start.4 = (bf16[336]{0:T(512)(128)(2,1)S(1)}, bf16[336]{0:T(512)(128)(2,1)}, u32[]{:S(2)}) copy-start(bf16[336]{0:T(512)(128)(2,1)} %param.18) | copy-start | bytes 2020
  2.5 2.9 %copy-start.5 = (bf16[336]{0:T(512)(128)(2,1)S(1)}, bf16[336]{0:T(512)(128)(2,1)}, u32[]{:S(2)}) copy-start(bf16[336]{0:T(512)(128)(2,1)} %param.25) | copy-start | bytes 2020
  2.6 2.9 %copy-start.6 = (bf16[336]{0:T(512)(128)(2,1)S(1)}, bf16[336]{0:T(512)(128)(2,1)}, u32[]{:S(2)}) copy-start(bf16[336]{0:T(512)(128)(2,1)} %param.26) | copy-start | bytes 2020
  2.6 2.9 %copy-start.7 = (bf16[336]{0:T(512)(128)(2,1)S(1)}, bf16[336]{0:T(512)(128)(2,1)}, u32[]{:S(2)}) copy-start(bf16[336]{0:T(512)(128)(2,1)} %param.27) | copy-start | bytes 2020
  2.6 3.6 %copy-start.2 = (f32[128]{0:T(128)S(1)}, f32[128]{0:T(128)}, u32[]{:S(2)}) copy-start(f32[128]{0:T(128)} %param.22) | copy-start | bytes 1540
  2.6 3.6 %copy-start.3 = (f32[128]{0:T(128)S(1)}, f32[128]{0:T(128)}, u32[]{:S(2)}) copy-start(f32[128]{0:T(128)} %param.23) | copy-start | bytes 1540
  6.8 119.3 %copy-start.8 = (s32[2]{0:T(128)S(1)}, s32[2]{0:T(128)}, u32[]{:S(2)}) copy-start(s32[2]{0:T(128)} %param.16) | copy-start | bytes 28
  6.8 120.1 %copy-start.9 = (s32[2]{0:T(128)S(1)}, s32[2]{0:T(128)}, u32[]{:S(2)}) copy-start(s32[2]{0:T(128)} %param.17) | copy-start | bytes 28

commit v2 on v1

--- a/solution.py
+++ b/solution.py
@@ -74,9 +74,9 @@
 
 
 def kernel(
-    hid, wp, wo, gp, hg, cos_t, sin_t, out,
+    hid, wq, wk, wv, wo, gp, hg, cos_t, sin_t, out,
     xb, wb, wob, gb, gfull, qs, ks, vs, ms, mb, bp, bs, br, hs, sr, rs, rr,
-    ws1, ws2, ws3, w_r, xs1, xs2, xs3, xs4, x_r, os_, o_r, gs, g_r, mss, m_r,
+    ws1, ws2, ws3, w_r, xs1, xz, xs2, xs3, xs4, x_r, os_, o_r, gs, g_r, mss, mz, m_r,
     b_s, b_r, ss, s_r, rss, r_r,
 ):
     sec = lax.axis_index("section")
@@ -87,7 +87,7 @@
     width = hid.shape[2]
     n_z = 4
     n_s = 8
-    rows = wp.shape[1]
+    rows = wq.shape[0]
     part = tok // 4
     tokens = n_s * tok
     half = tokens // 2
@@ -119,38 +119,59 @@
     def x_part(m):
         return hid.at[m, pl.ds(pl.multiple_of(sec * part, 16), part), :]
 
+    def w_pieces(h):
+        at = w_at(seq)
+        return (
+            (wq.at[:, pl.ds(h * 2 * HD, 2 * HD)], at.at[:, pl.ds(0, 2 * HD)]),
+            (wk.at[:, pl.ds(h * HD, HD)], at.at[:, pl.ds(2 * HD, HD)]),
+            (wv.at[:, pl.ds(h * HD, HD)], at.at[:, pl.ds(3 * HD, HD)]),
+        )
+
     def w_send(h):
         zd = 2 * g + h
-        cp = remote(wp.at[h], w_at(seq), ws1.at[h], w_r.at[seq], sec, 2 * zd + y)
+        made = []
+        for i, (src, dst) in enumerate(w_pieces(h)):
+            made.append((zd != z, remote(src, dst, ws1.at[h, i], w_r.at[seq], sec, 2 * zd + y)))
 
         @pl.when(zd != z)
         def _():
-            cp.start()
+            for _, cp in made:
+                cp.start()
 
         @pl.when(zd == z)
         def _():
-            pltpu.make_async_copy(wp.at[h], w_at(seq), w_r.at[seq]).start()
-
-        return zd != z, cp
+            for src, dst in w_pieces(h):
+                pltpu.make_async_copy(src, dst, w_r.at[seq]).start()
+
+        return made
 
     pltpu.make_async_copy(x_part(y), xb.at[seq, sec], x_r.at[seq, sec]).start()
-    cp = remote(x_part(1 - y), xb.at[seq, sec], xs1.at[1], x_r.at[seq, sec], sec, 2 * z + 1 - y)
+    cp = remote(x_part(1 - y), xb.at[seq, sec], xs1, x_r.at[seq, sec], sec, 2 * z + 1 - y)
     cp.start()
     sends.append(cp)
-    cond_sends = [w_send(0), w_send(1)]
-    for k in range(1, n_z):
-        zd = (z + k) % n_z
-        for j in range(2):
-            m = (y + j) % 2
-            cp = remote(
-                x_part(m), xb.at[seq, sec], xs1.at[2 * k + j], x_r.at[seq, sec], sec, 2 * zd + m
-            )
-            cp.start()
-            sends.append(cp)
+    cond_sends = w_send(0) + w_send(1)
+
+    mid = (z % 2 + z // 2) % 2
+    far2 = (z + 2) % n_z
+    planes = (
+        z,
+        z + 1 - 2 * (z % 2),
+        mid * (n_z - 1 - z) + (1 - mid) * far2,
+        (1 - mid) * (n_z - 1 - z) + mid * far2,
+    )
+    onward = (None, z + 2 * (z % 2) - 1, z + 2 * (z // 2) - 1, z + 2 * (z // 2) - 1)
+
+    def pass_on(k, src, send_sems, r_sem, c2):
+        targets = (z + 1, z - 1) if k == 0 else (onward[k],)
+        for t, zn in enumerate(targets):
+            ok = (zn >= 0) & (zn < n_z)
+            cp = remote(src, src, send_sems.at[t], r_sem, c2, 2 * ((zn + n_z) % n_z) + y)
+            pl.when(ok)(cp.start)
+            cond_sends.append((ok, cp))
 
     w_home = g == z // 2
     for k in range(n_z):
-        z2 = (z - k + n_z) % n_z
+        z2 = planes[k]
         s2 = 2 * z2 + y
         yf = remote(w_at(s2), w_at(s2), ws2.at[k], w_r.at[s2], sec, 2 * z + 1 - y)
         cf = remote(w_at(s2), w_at(s2), ws3.at[k], w_r.at[s2], csec, seq)
@@ -164,34 +185,25 @@
         cond_sends += [(w_home, yf), (w_home, cf)]
         for j in range(2):
             s2 = 2 * z2 + (y + j) % 2
-            arrived(xb.at[s2, sec], x_r.at[s2, sec])
+            here = xb.at[s2, sec]
+            arrived(here, x_r.at[s2, sec])
             i = 2 * k + j
-            xf = remote(
-                xb.at[s2, sec], xb.at[s2, sec], xs2.at[i], x_r.at[s2, sec], xsec, seq
-            )
+            pass_on(k, here, xz.at[i], x_r.at[s2, sec], sec)
+            xf = remote(here, here, xs2.at[i], x_r.at[s2, sec], xsec, seq)
             xf.start()
-            cx = remote(
-                xb.at[s2, sec], xb.at[s2, sec], xs3.at[i], x_r.at[s2, sec], csec, seq
-            )
+            cx = remote(here, here, xs3.at[i], x_r.at[s2, sec], csec, seq)
             cx.start()
             sends += [xf, cx]
-    own_o = wob.at[y, pl.ds(pl.multiple_of(g * 512, 512), 512), :]
-    i = 0
-    for dy in range(2):
-        for dg in range(2):
-            if dy == 0 and dg == 0:
-                pltpu.make_async_copy(wo, own_o, o_r.at[2 * y + g]).start()
-            else:
-                cp = remote(
-                    wo, own_o, os_.at[i], o_r.at[2 * y + g],
-                    x * 2 + (g + dg) % 2, 2 * z + (y + dy) % 2,
-                )
-                cp.start()
-                sends.append(cp)
-            i += 1
+    def o_at(y2, g2):
+        return wob.at[y2, pl.ds(pl.multiple_of(g2 * 512, 512), 512), :]
+
+    pltpu.make_async_copy(wo, o_at(y, g), o_r.at[2 * y + g]).start()
+    for i, (c2, s2) in enumerate(((csec, seq), (sec, 2 * z + 1 - y))):
+        cp = remote(wo, o_at(y, g), os_.at[i], o_r.at[2 * y + g], c2, s2)
+        cp.start()
+        sends.append(cp)
     for k in range(n_z):
-        z2 = (z - k + n_z) % n_z
-        s2 = 2 * z2 + 1 - y
+        s2 = 2 * planes[k] + 1 - y
         cf = remote(w_at(s2), w_at(s2), ws3.at[n_z + k], w_r.at[s2], csec, seq)
 
         @pl.when(w_home)
@@ -211,7 +223,7 @@
         gfull[:, s2 * rows : (s2 + 1) * rows] = gb[s2]
     for k in range(n_z):
         for j in range(2):
-            s2 = 2 * ((z - k + n_z) % n_z) + (y + j) % 2
+            s2 = 2 * planes[k] + (y + j) % 2
             arrived(xb.at[s2, xsec], x_r.at[s2, xsec])
             cp = remote(
                 xb.at[s2, xsec], xb.at[s2, xsec], xs4.at[2 * k + j], x_r.at[s2, xsec], csec, seq
@@ -220,7 +232,8 @@
             sends.append(cp)
 
     def project(k, carry):
-        s2 = 2 * ((z - k // 2 + n_z) % n_z) + (y + k % 2) % 2
+        k1, k0 = k // 4, (k // 2) % 2
+        s2 = 2 * (2 * ((z // 2 + k1) % 2) + (z + k0) % 2) + (y + k % 2) % 2
         arrived(xb.at[s2, csec], x_r.at[s2, csec])
         c3 = (csec + 2) % 4
         arrived(xb.at[s2, c3], x_r.at[s2, c3])
@@ -244,10 +257,14 @@
 
     lax.fori_loop(0, n_s, project, 0)
 
+    arrived(o_at(1 - y, g), o_r.at[2 * (1 - y) + g])
+    cp = remote(
+        o_at(1 - y, g), o_at(1 - y, g), os_.at[2], o_r.at[2 * (1 - y) + g], csec, seq
+    )
+    cp.start()
+    sends.append(cp)
+
     head_id = 2 * z + g
-
-    def m_slot(h):
-        return mb.at[h]
 
     blk = tokens // 4
     for qb in range(4):
@@ -267,14 +284,15 @@
         if qb % 2 == 1:
             gd = qb // 2
             src = ms.at[pl.ds(gd * half, half), :]
-            for k in range(1, n_z):
-                zd = (z + k) % n_z
+            for t, zn in enumerate((z + 1, z - 1)):
+                ok = (zn >= 0) & (zn < n_z)
                 cp = remote(
-                    src, m_slot(head_id), mss.at[gd, k], m_r.at[head_id], 2 * x + gd, 2 * zd + y
+                    src, mb.at[head_id], mss.at[gd, t], m_r.at[head_id],
+                    2 * x + gd, 2 * ((zn + n_z) % n_z) + y,
                 )
-                cp.start()
-                sends.append(cp)
-            cp = remote(src, m_slot(head_id), mss.at[gd, 0], m_r.at[head_id], csec, seq)
+                pl.when(ok)(cp.start)
+                cond_sends.append((ok, cp))
+            cp = remote(src, mb.at[head_id], mss.at[gd, 2], m_r.at[head_id], csec, seq)
 
             @pl.when(g != gd)
             def _():
@@ -282,9 +300,17 @@
 
             @pl.when(g == gd)
             def _():
-                pltpu.make_async_copy(src, m_slot(head_id), m_r.at[head_id]).start()
+                pltpu.make_async_copy(src, mb.at[head_id], m_r.at[head_id]).start()
 
             cond_sends.append((g != gd, cp))
+    for k in range(1, n_z):
+        for j in range(2):
+            h = 2 * planes[k] + j
+            arrived(mb.at[h], m_r.at[h])
+            pass_on(k, mb.at[h], mz.at[2 * k + j], m_r.at[h], sec)
+    for j in range(2):
+        h = 2 * z + j
+        arrived(mb.at[h], m_r.at[h])
 
     first = 4 * g + 2 * x
     for zz in range(n_z):
@@ -299,25 +325,24 @@
                         jnp.float32
                     )
 
-    for i in range(4):
-        o_here = wob.at[i // 2, pl.ds((i % 2) * 512, 512), :]
-        arrived(o_here, o_r.at[i])
-    for h in range(n_s):
-        arrived(m_slot(h), m_r.at[h])
-    mixed = jnp.concatenate([mb[h] for h in range(n_s)], axis=1)
-    for yc in range(2):
-        bp[yc] = jnp.dot(mixed, wob[yc], preferred_element_type=jnp.float32)
+    arrived(o_at(y, g), o_r.at[2 * y + g])
+    for y2 in range(2):
+        arrived(o_at(y2, 1 - g), o_r.at[2 * y2 + 1 - g])
     away = pl.ds(pl.multiple_of((1 - x) * quarter, quarter), quarter)
     home = pl.ds(pl.multiple_of(x * quarter, quarter), quarter)
+    mixed = jnp.concatenate([mb[h, away, :] for h in range(n_s)], axis=1)
     for yc in range(2):
-        bs[yc] = bp[yc, away, :].astype(jnp.bfloat16)
+        bs[yc] = jnp.dot(mixed, wob[yc], preferred_element_type=jnp.float32).astype(jnp.bfloat16)
     cp = remote(bs, br, b_s, b_r, xsec, seq)
     cp.start()
     sends.append(cp)
+    mixed = jnp.concatenate([mb[h, home, :] for h in range(n_s)], axis=1)
+    for yc in range(2):
+        bp[yc] = jnp.dot(mixed, wob[yc], preferred_element_type=jnp.float32)
     arrived(br, b_r)
     cols = [jnp.zeros((quarter, 1), jnp.float32)] * 6
     for yc in range(2):
-        b = bp[yc, home, :] + br[yc].astype(jnp.float32)
+        b = bp[yc] + br[yc].astype(jnp.float32)
         h = hs[yc]
         gains = gb[2 * z + yc]
         post = gains[1:2, :]
@@ -386,14 +411,6 @@
     rows = w_query.shape[0]
     tokens = tok * lax.axis_size("seq")
     quarter = tokens // 4
-    wp = jnp.concatenate(
-        [
-            w_query.reshape(rows, 2, GROUP * HD),
-            w_key.reshape(rows, 2, HD),
-            w_value.reshape(rows, 2, HD),
-        ],
-        axis=2,
-    ).transpose(1, 0, 2)
     gp = jnp.stack([in_gain, post_gain, final_gain, value_head] * 2).astype(jnp.float32)
     hg = jnp.stack([query_gain, key_gain] * 4)
     cos_t, sin_t = rope_tables(tokens)
@@ -403,25 +420,26 @@
     raw = pl.pallas_call(
         kernel,
         out_shape=jax.ShapeDtypeStruct((8, quarter), f32),
-        in_specs=[pl.BlockSpec(memory_space=pltpu.VMEM)] * 7,
+        in_specs=[pl.BlockSpec(memory_space=pl.ANY)] * 5
+        + [pl.BlockSpec(memory_space=pltpu.VMEM)] * 4,
         out_specs=pl.BlockSpec(memory_space=pltpu.VMEM),
         scratch_shapes=[
             V((8, 4, tok // 4, width), bf), V((width, 512), bf), V((2, 1024, rows), bf),
             V((8, 8, rows), f32), V((8, width), f32),
             V((tokens, HD), bf), V((tokens, HD), bf), V((tokens, HD), bf), V((tokens, HD), bf),
-            V((8, tokens // 2, HD), bf), V((2, tokens // 2, rows), f32),
+            V((8, tokens // 2, HD), bf), V((2, quarter, rows), f32),
             V((2, quarter, rows), bf), V((2, quarter, rows), bf), V((2, quarter, rows), f32),
             V((4, 8, quarter), f32), V((8, 128), f32), V((8, 8, quarter), f32),
-            dma((2,)), dma((4,)), dma((8,)), dma((8,)),
-            dma((8,)), dma((8,)), dma((8,)), dma((8,)), dma((8, 4)),
-            dma((4,)), dma((4,)), dma((8,)), dma((8,)), dma((2, 4)), dma((8,)),
+            dma((2, 3)), dma((4,)), dma((8,)), dma((8,)),
+            dma, dma((8, 2)), dma((8,)), dma((8,)), dma((8,)), dma((8, 4)),
+            dma((4,)), dma((4,)), dma((8,)), dma((8,)), dma((2, 3)), dma((8, 2)), dma((8,)),
             dma, dma, dma((4,)), dma((4,)), dma((8,)), dma((8,)),
         ],
         compiler_params=pltpu.CompilerParams(
             has_side_effects=True, vmem_limit_bytes=60 * 1024 * 1024
         ),
         name="whole_layer",
-    )(hidden, wp, w_out, gp, hg, cos_t, sin_t)
+    )(hidden, w_query, w_key, w_value, w_out, gp, hg, cos_t, sin_t)
     raw = raw.reshape(micro_count, tokens)
     pos = jnp.arange(tokens, dtype=jnp.int32)[None, :]
     full = jnp.where(pos < lengths[:, None], raw, 0.0)

time: 129 us -> 115 us (0.89)
  Pallas kernels: 119 us -> 104 us
  local copies, waits for them, and re-layouts: 5.66 us -> 7.22 us
    pallas_call x1, Pallas kernels: 119 us -> 104 us  [fused(): pl.pallas_call(kernel, out_shape=jax.ShapeDtypeStruct((8, quarter), f32),...]
    another operation x5, local copies, waits for them, and re-layouts: 0.06 us -> 2.77 us  [fused(): jnp.stack([in_gain, post_gain, final_gain, value_head] * 2)]
    reshape x2 -> x0, local copies, waits for them, and re-layouts: 2 us -> none  [the longest x1 1.03 us: fused(): w_query.reshape(rows, 2, GROUP * HD)]
where the time goes in v2:
time: 115 us
  Pallas kernels  104 us (90%)
  local copies, waits for them, and re-layouts  7.22 us (6%)
  other arithmetic  2.75 us (2%)
    pallas_call x1, Pallas kernels, fused(): pl.pallas_call(kernel, out_shape=jax.ShapeDtypeStruct((8, quarter), f32),...  104 us
    another operation x5, local copies, waits for them, and re-layouts, fused(): jnp.stack([in_gain, post_gain, final_gain, value_head] * 2)  2.77 us

profile of v2, /device:TPU:0, one launch (start us, length us, event | category | flops | bytes accessed | tf_op | source)
XLA Modules:
  0.0 115.1 jit_solution(11392406682988768090)
XLA Ops:
  0.6 1.9 %copy.17.wo = bf16[512,336]{1,0:T(8,128)(2,1)} copy(bf16[512,336]{0,1:T(8,128)(2,1)} %param.24) | data formatting | bytes 688128 | tf_op args[9]
  2.5 0.7 stack.16
  3.2 0.7 stack.17
  3.9 0.7 stack.36
  4.6 0.7 stack.37
  5.3 0.6 convert_element_type.3.gp
  5.9 1.4 %stack.41.hg = f32[8,128]{1,0:T(8,128)} concatenate(f32[1,128]{1,0:T(1,128)} %bitcast.2, f32[1,128]{1,0:T(1,128)} %bitcast.6, f32[1,128]{1,0:T(1,128)} %bitcast.3, f32[1,128]{1,0:T(1,128)} %bitcast.7, f32[1,128]{1,0:T(1,128)} %bitcast.4, f32[1,128]{1,0:T(1,128)} %bitcast.8, f32[1,128]{1,0:T(1,128)} %bitcast.5, f32[1,128]{1,0:T(1,128)} %bitcast.9), dimensions={0} | concatenate | bytes 8192 | tf_op jit(solution)/shard_map/stack | solution.py:415
  7.3 0.0 copy-start
  7.3 0.0 copy-start.1
  7.3 104.4 %whole_layer.1 = f32[8,256]{1,0:T(8,128)} custom-call(bf16[2,128,2688]{2,1,0:T(8,128)(2,1)} %hid.1, bf16[336,512]{1,0:T(8,128)(2,1)} %wq.1, bf16[336,256]{1,0:T(8,128)(2,1)} %wk.1, bf16[336,256]{1,0:T(8,128)(2,1)} %wv.1, bf16[512,336]{1,0:T(8,128)(2,1)} %copy.17.wo, f32[8,336]{1,0:T(8,128)} %convert_element_type.3.gp, f32[8,128]{1,0:T(8,128)} %stack.41.hg, ...), custom_call_target="tpu_custom_call" | custom-call | tf_op jit(solution)/shard_map/whole_layer/pallas_call | solution.py:420
  111.8 0.7 reshape.16
  112.5 0.0 copy-done
  112.5 0.6 compare_select_fusion
  113.1 0.1 lt.52
  113.2 0.1 lt.53
  113.3 0.0 copy-done.1
  113.3 0.1 eq.16
  113.4 0.1 eq.17
  113.5 0.9 select_reduce_fusion
  114.3 0.1 reduce_sum.14
  114.4 0.6 reduce_sum.18
  (4 shorter events, 0.1 us)
Async XLA Ops:
  7.3 105.2 %copy-start = (s32[2]{0:T(128)S(1)}, s32[2]{0:T(128)}, u32[]{:S(2)}) copy-start(s32[2]{0:T(128)} %param.16) | copy-start | bytes 28
  7.3 106.0 %copy-start.1 = (s32[2]{0:T(128)S(1)}, s32[2]{0:T(128)}, u32[]{:S(2)}) copy-start(s32[2]{0:T(128)} %param.17) | copy-start | bytes 28

commit v3 on v2

--- a/solution.py
+++ b/solution.py
@@ -73,8 +73,15 @@
 MESH = pl.DeviceIdType.MESH
 
 
+def by_rows(a, b):
+    return lax.dot_general(
+        a, b, (((1,), (1,)), ((), ())), preferred_element_type=jnp.float32
+    )
+
+
 def kernel(
-    hid, wq, wk, wv, wo, gp, hg, cos_t, sin_t, out,
+    hid, wq, wk, wv, wo, g0, g1, g2, g3, qg, kg, cos_t, sin_t, out,
+    gp,
     xb, wb, wob, gb, gfull, qs, ks, vs, ms, mb, bp, bs, br, hs, sr, rs, rr,
     ws1, ws2, ws3, w_r, xs1, xz, xs2, xs3, xs4, x_r, os_, o_r, gs, g_r, mss, mz, m_r,
     b_s, b_r, ss, s_r, rss, r_r,
@@ -108,6 +115,8 @@
         return wb.at[pl.ds(pl.multiple_of(s2 * rows, 16), rows), :]
 
     sends = []
+    for i, ref in enumerate((g0, g1, g2, g3)):
+        gp[i : i + 1, :] = ref[...].astype(jnp.float32)
     for k in range(1, n_s):
         s2 = (seq + k) % n_s
         cp = remote(gp, gb.at[seq], gs.at[k], g_r.at[seq], sec, s2)
@@ -195,7 +204,7 @@
             cx.start()
             sends += [xf, cx]
     def o_at(y2, g2):
-        return wob.at[y2, pl.ds(pl.multiple_of(g2 * 512, 512), 512), :]
+        return wob.at[y2, :, pl.ds(pl.multiple_of(g2 * 512, 512), 512)]
 
     pltpu.make_async_copy(wo, o_at(y, g), o_r.at[2 * y + g]).start()
     for i, (c2, s2) in enumerate(((csec, seq), (sec, 2 * z + 1 - y))):
@@ -250,8 +259,8 @@
             return u * cos_b + pltpu.roll(u, HD // 2, 1) * sin_b
 
         q = jnp.where(g == 0, acc[:, :HD], acc[:, HD : 2 * HD])
-        qs[here, :] = (turned(q, hg[0:1, :]) * query_scale).astype(jnp.bfloat16)
-        ks[here, :] = turned(acc[:, 2 * HD : 3 * HD], hg[1:2, :]).astype(jnp.bfloat16)
+        qs[here, :] = (turned(q, qg[...]) * query_scale).astype(jnp.bfloat16)
+        ks[here, :] = turned(acc[:, 2 * HD : 3 * HD], kg[...]).astype(jnp.bfloat16)
         vs[here, :] = acc[:, 3 * HD :].astype(jnp.bfloat16)
         return carry
 
@@ -265,6 +274,10 @@
     sends.append(cp)
 
     head_id = 2 * z + g
+
+    def pass_copy(k, j, h):
+        zn = (onward[k] + n_z) % n_z
+        return remote(mb.at[h], mb.at[h], mz.at[2 * k + j, 0], m_r.at[h], sec, 2 * zn + y)
 
     blk = tokens // 4
     for qb in range(4):
@@ -303,11 +316,25 @@
                 pltpu.make_async_copy(src, mb.at[head_id], m_r.at[head_id]).start()
 
             cond_sends.append((g != gd, cp))
+        if qb > 1:
+            steps = ((g == 0, (1,)),) if qb == 2 else ((g == 0, (2, 3)), (g == 1, (1, 2, 3)))
+            for cond, ks_ in steps:
+
+                @pl.when(cond)
+                def _():
+                    for k in ks_:
+                        for j in range(2):
+                            h = 2 * planes[k] + j
+                            arrived(mb.at[h], m_r.at[h])
+                            zn = onward[k]
+                            ok = (zn >= 0) & (zn < n_z)
+                            cp = pass_copy(k, j, h)
+                            pl.when(ok)(cp.start)
+
     for k in range(1, n_z):
         for j in range(2):
-            h = 2 * planes[k] + j
-            arrived(mb.at[h], m_r.at[h])
-            pass_on(k, mb.at[h], mz.at[2 * k + j], m_r.at[h], sec)
+            zn = onward[k]
+            cond_sends.append(((zn >= 0) & (zn < n_z), pass_copy(k, j, 2 * planes[k] + j)))
     for j in range(2):
         h = 2 * z + j
         arrived(mb.at[h], m_r.at[h])
@@ -332,13 +359,13 @@
     home = pl.ds(pl.multiple_of(x * quarter, quarter), quarter)
     mixed = jnp.concatenate([mb[h, away, :] for h in range(n_s)], axis=1)
     for yc in range(2):
-        bs[yc] = jnp.dot(mixed, wob[yc], preferred_element_type=jnp.float32).astype(jnp.bfloat16)
+        bs[yc] = by_rows(mixed, wob[yc]).astype(jnp.bfloat16)
     cp = remote(bs, br, b_s, b_r, xsec, seq)
     cp.start()
     sends.append(cp)
     mixed = jnp.concatenate([mb[h, home, :] for h in range(n_s)], axis=1)
     for yc in range(2):
-        bp[yc] = jnp.dot(mixed, wob[yc], preferred_element_type=jnp.float32)
+        bp[yc] = by_rows(mixed, wob[yc])
     arrived(br, b_r)
     cols = [jnp.zeros((quarter, 1), jnp.float32)] * 6
     for yc in range(2):
@@ -411,8 +438,10 @@
     rows = w_query.shape[0]
     tokens = tok * lax.axis_size("seq")
     quarter = tokens // 4
-    gp = jnp.stack([in_gain, post_gain, final_gain, value_head] * 2).astype(jnp.float32)
-    hg = jnp.stack([query_gain, key_gain] * 4)
+    vectors = [
+        v.reshape(1, -1)
+        for v in (in_gain, post_gain, final_gain, value_head, query_gain, key_gain)
+    ]
     cos_t, sin_t = rope_tables(tokens)
     bf, f32 = jnp.bfloat16, jnp.float32
     V = pltpu.VMEM
@@ -421,10 +450,11 @@
         kernel,
         out_shape=jax.ShapeDtypeStruct((8, quarter), f32),
         in_specs=[pl.BlockSpec(memory_space=pl.ANY)] * 5
-        + [pl.BlockSpec(memory_space=pltpu.VMEM)] * 4,
+        + [pl.BlockSpec(memory_space=pltpu.VMEM)] * 8,
         out_specs=pl.BlockSpec(memory_space=pltpu.VMEM),
         scratch_shapes=[
-            V((8, 4, tok // 4, width), bf), V((width, 512), bf), V((2, 1024, rows), bf),
+            V((8, rows), f32),
+            V((8, 4, tok // 4, width), bf), V((width, 512), bf), V((2, rows, 1024), bf),
             V((8, 8, rows), f32), V((8, width), f32),
             V((tokens, HD), bf), V((tokens, HD), bf), V((tokens, HD), bf), V((tokens, HD), bf),
             V((8, tokens // 2, HD), bf), V((2, quarter, rows), f32),
@@ -439,7 +469,7 @@
             has_side_effects=True, vmem_limit_bytes=60 * 1024 * 1024
         ),
         name="whole_layer",
-    )(hidden, w_query, w_key, w_value, w_out, gp, hg, cos_t, sin_t)
+    )(hidden, w_query, w_key, w_value, w_out.T, *vectors, cos_t, sin_t)
     raw = raw.reshape(micro_count, tokens)
     pos = jnp.arange(tokens, dtype=jnp.int32)[None, :]
     full = jnp.where(pos < lengths[:, None], raw, 0.0)

time: 115 us -> 117 us (1.017)
  Pallas kernels: 104 us -> 108 us
    reshape x0 -> x4, local copies, waits for them, and re-layouts: none -> 4.99 us  [fused(): v.reshape(1, -1)]
    another operation x6 -> x0, local copies, waits for them, and re-layouts: 4.21 us -> none  [the longest x5 2.77 us: fused(): jnp.stack([in_gain, post_gain, final_gain, value_head] * 2)]
    pallas_call x1, Pallas kernels: 104 us -> 108 us  [fused(): pl.pallas_call(kernel, out_shape=jax.ShapeDtypeStruct((8, quarter), f32),...]
    unnamed x5 -> x4, local copies, waits for them, and re-layouts: 1.9 us -> 0.01 us
where the time goes in v3:
time: 117 us
  Pallas kernels  108 us (92%)
  local copies, waits for them, and re-layouts  6.11 us (5%)
  other arithmetic  2.15 us (2%)
    pallas_call x1, Pallas kernels, fused(): pl.pallas_call(kernel, out_shape=jax.ShapeDtypeStruct((8, quarter), f32),...  108 us
    reshape x4, local copies, waits for them, and re-layouts, fused(): v.reshape(1, -1)  4.99 us

profile of v3, /device:TPU:0, one launch (start us, length us, event | category | flops | bytes accessed | tf_op | source)
XLA Modules:
  0.0 116.8 jit_solution(8339551667096916191)
XLA Ops:
  0.6 1.3 %reshape.34.g0 = bf16[1,336]{1,0:T(2,128)(2,1)} reshape(bf16[336]{0:T(512)(128)(2,1)} %param.18) | data formatting | bytes 1344 | tf_op jit(solution)/shard_map/reshape | solution.py:442
  1.9 1.2 %reshape.35.g1 = bf16[1,336]{1,0:T(2,128)(2,1)} reshape(bf16[336]{0:T(512)(128)(2,1)} %param.25) | data formatting | bytes 1344 | tf_op jit(solution)/shard_map/reshape | solution.py:442
  3.1 1.3 %reshape.36.g2 = bf16[1,336]{1,0:T(2,128)(2,1)} reshape(bf16[336]{0:T(512)(128)(2,1)} %param.26) | data formatting | bytes 1344 | tf_op jit(solution)/shard_map/reshape | solution.py:442
  4.4 1.2 %reshape.37.g3 = bf16[1,336]{1,0:T(2,128)(2,1)} reshape(bf16[336]{0:T(512)(128)(2,1)} %param.27) | data formatting | bytes 1344 | tf_op jit(solution)/shard_map/reshape | solution.py:442
  5.6 0.0 copy-start
  5.6 0.0 copy-start.1
  5.6 107.9 %whole_layer.1 = f32[8,256]{1,0:T(8,128)} custom-call(bf16[2,128,2688]{2,1,0:T(8,128)(2,1)} %hid.1, bf16[336,512]{1,0:T(8,128)(2,1)} %wq.1, bf16[336,256]{1,0:T(8,128)(2,1)} %wk.1, bf16[336,256]{1,0:T(8,128)(2,1)} %wv.1, bf16[336,512]{1,0:T(8,128)(2,1)} %bitcast.3, bf16[1,336]{1,0:T(2,128)(2,1)} %reshape.34.g0, bf16[1,336]{1,0:T(2,128)(2,1)} %reshape.35.g1, ...), custom_call_target="tpu_custom_call" | custom-call | tf_op jit(solution)/shard_map/whole_layer/pallas_call | solution.py:449
  113.5 0.7 reshape.40
  114.2 0.0 copy-done
  114.2 0.6 compare_select_fusion
  114.9 0.0 copy-done.1
  114.9 0.1 eq.16
  115.0 0.1 eq.17
  115.0 0.1 lt.52
  115.1 0.1 lt.53
  115.2 0.9 select_reduce_fusion
  116.1 0.1 reduce_sum.14
  116.2 0.6 reduce_sum.18
  (3 shorter events, 0.0 us)
Async XLA Ops:
  5.6 108.6 %copy-start = (s32[2]{0:T(128)S(1)}, s32[2]{0:T(128)}, u32[]{:S(2)}) copy-start(s32[2]{0:T(128)} %param.16) | copy-start | bytes 28
  5.6 109.3 %copy-start.1 = (s32[2]{0:T(128)S(1)}, s32[2]{0:T(128)}, u32[]{:S(2)}) copy-start(s32[2]{0:T(128)} %param.17) | copy-start | bytes 28

commit v4 on v3

--- a/solution.py
+++ b/solution.py
@@ -116,7 +116,7 @@
 
     sends = []
     for i, ref in enumerate((g0, g1, g2, g3)):
-        gp[i : i + 1, :] = ref[...].astype(jnp.float32)
+        gp[i : i + 1, :] = ref[...].astype(jnp.float32).reshape(1, rows)
     for k in range(1, n_s):
         s2 = (seq + k) % n_s
         cp = remote(gp, gb.at[seq], gs.at[k], g_r.at[seq], sec, s2)
@@ -274,10 +274,6 @@
     sends.append(cp)
 
     head_id = 2 * z + g
-
-    def pass_copy(k, j, h):
-        zn = (onward[k] + n_z) % n_z
-        return remote(mb.at[h], mb.at[h], mz.at[2 * k + j, 0], m_r.at[h], sec, 2 * zn + y)
 
     blk = tokens // 4
     for qb in range(4):
@@ -316,25 +312,11 @@
                 pltpu.make_async_copy(src, mb.at[head_id], m_r.at[head_id]).start()
 
             cond_sends.append((g != gd, cp))
-        if qb > 1:
-            steps = ((g == 0, (1,)),) if qb == 2 else ((g == 0, (2, 3)), (g == 1, (1, 2, 3)))
-            for cond, ks_ in steps:
-
-                @pl.when(cond)
-                def _():
-                    for k in ks_:
-                        for j in range(2):
-                            h = 2 * planes[k] + j
-                            arrived(mb.at[h], m_r.at[h])
-                            zn = onward[k]
-                            ok = (zn >= 0) & (zn < n_z)
-                            cp = pass_copy(k, j, h)
-                            pl.when(ok)(cp.start)
-
     for k in range(1, n_z):
         for j in range(2):
-            zn = onward[k]
-            cond_sends.append(((zn >= 0) & (zn < n_z), pass_copy(k, j, 2 * planes[k] + j)))
+            h = 2 * planes[k] + j
+            arrived(mb.at[h], m_r.at[h])
+            pass_on(k, mb.at[h], mz.at[2 * k + j], m_r.at[h], sec)
     for j in range(2):
         h = 2 * z + j
         arrived(mb.at[h], m_r.at[h])
@@ -439,8 +421,8 @@
     tokens = tok * lax.axis_size("seq")
     quarter = tokens // 4
     vectors = [
-        v.reshape(1, -1)
-        for v in (in_gain, post_gain, final_gain, value_head, query_gain, key_gain)
+        in_gain, post_gain, final_gain, value_head,
+        query_gain.reshape(1, -1), key_gain.reshape(1, -1),
     ]
     cos_t, sin_t = rope_tables(tokens)
     bf, f32 = jnp.bfloat16, jnp.float32

time: 117 us -> 110 us (0.940)
  local copies, waits for them, and re-layouts: 6.11 us -> 2.43 us
  Pallas kernels: 108 us -> 105 us
    reshape x4 -> x0, local copies, waits for them, and re-layouts: 4.99 us -> none  [fused(): v.reshape(1, -1)]
    pallas_call x1, Pallas kernels: 108 us -> 105 us  [fused(): pl.pallas_call(kernel, out_shape=jax.ShapeDtypeStruct((8, quarter), f32),...]
where the time goes in v4:
time: 110 us
  Pallas kernels  105 us (95%)
  local copies, waits for them, and re-layouts  2.43 us (2%)
  other arithmetic  2.15 us (2%)
    pallas_call x1, Pallas kernels, fused(): pl.pallas_call(kernel, out_shape=jax.ShapeDtypeStruct((8, quarter), f32),...  105 us

profile of v4, /device:TPU:0, one launch (start us, length us, event | category | flops | bytes accessed | tf_op | source)
XLA Modules:
  0.0 109.9 jit_solution(237688115407909866)
XLA Ops:
  0.6 0.7 eq.16
  1.4 0.1 eq.17
  1.4 0.7 lt.52
  2.2 0.1 lt.53
  2.3 0.0 copy-start
  2.3 104.7 %whole_layer.1 = f32[8,256]{1,0:T(8,128)} custom-call(bf16[2,128,2688]{2,1,0:T(8,128)(2,1)} %hid.1, bf16[336,512]{1,0:T(8,128)(2,1)} %wq.1, bf16[336,256]{1,0:T(8,128)(2,1)} %wk.1, bf16[336,256]{1,0:T(8,128)(2,1)} %wv.1, bf16[336,512]{1,0:T(8,128)(2,1)} %bitcast.3, bf16[336]{0:T(512)(128)(2,1)} %g0.1, bf16[336]{0:T(512)(128)(2,1)} %g1.1, bf16[336]{0:T(512)(128)(2,1)} %g2.1, ...), custom_call_target="tpu_custom_call" | custom-call | tf_op jit(solution)/shard_map/whole_layer/pallas_call | solution.py:431
  107.0 0.9 select_reduce_fusion
  107.8 0.7 reshape.24
  108.6 0.0 copy-done
  108.6 0.6 compare_select_fusion
  109.2 0.1 reduce_sum.14
  109.3 0.6 reduce_sum.18
  (3 shorter events, 0.0 us)
Async XLA Ops:
  2.3 106.3 %copy-start = (s32[2]{0:T(128)S(1)}, s32[2]{0:T(128)}, u32[]{:S(2)}) copy-start(s32[2]{0:T(128)} %param.16) | copy-start | bytes 28
